TPU v7x, 512 devices: a whole 4x8x8 slice. The times are simulated.
512 devices in a mesh: ep: 64 (over x, z, core), tp: 8 (over y).
Axes of the slice: x: 4, y: 8, z: 8, core: 2. Of those that a mesh axis runs over, the one named last changes fastest.
Arguments:
- tokens: bfloat16 [2, 1024, 4096], P(None, 'ep', 'tp'), may hold values from -6 to 6
- routes: int32 [2, 1024, 8], P(None, 'ep'), may hold values from 0 to 63, all different within a row; in each aligned block of 16 rows (0 to 15, 16 to 31, ..., all dimensions but the last counted through in order) at most 4 rows name the same one
- route_weight: float32 [2, 1024, 8], P(None, 'ep'), may hold values from 0.1 to 0.6
- w_gate: bfloat16 [64, 4096, 1024], P('ep', None, 'tp'), may hold values from -0.09375 to 0.09375
- w_up: bfloat16 [64, 4096, 1024], P('ep', None, 'tp'), may hold values from -0.09375 to 0.09375
- w_down: bfloat16 [64, 1024, 4096], P('ep', 'tp'), may hold values from -0.1875 to 0.1875
Outputs:
- mixed: bfloat16 [2, 1024, 4096], P(None, 'ep', 'tp')
Inputs may be any that keep to these rules, and one draw needn't show every extreme that they name: `routes`: each row names 8 different experts. In each micro-batch, at most 4 of the rows of one index of ep name one expert, a bound that some of them reach.
All inputs are finite; a program needn't handle non-finite values.
Results may differ from a plain program's by a relative error of at most 0.015.
Values may be sent and summed in bfloat16 or wider, within the bound.
A program may use at most 64 MiB of HBM per device.

v0:
```python
import jax
import jax.numpy as jnp
from jax import lax
from jax.sharding import PartitionSpec as P


def slot_assignment(route_ids, experts, capacity):
    batches, tok_rows, per_token = route_ids.shape
    flat_ids = route_ids.reshape(batches, tok_rows * per_token)
    expert_indicator = (flat_ids[:, :, None] == jnp.arange(experts, dtype=jnp.int32)).astype(
        jnp.int32
    )
    running = jnp.cumsum(expert_indicator, axis=1) - 1
    slot_rank = jnp.sum(running * expert_indicator, axis=2)
    slot_ids = flat_ids * capacity + slot_rank
    return (slot_ids[:, :, None] == jnp.arange(experts * capacity, dtype=jnp.int32)).astype(
        jnp.int32
    )


def moe_layer(block_tokens, route_ids, routing_probability, w_gate, w_up, w_down):
    n_ep = lax.axis_size("ep")
    local_count = w_gate.shape[0]
    experts = local_count * n_ep
    batches, tok_rows, per_token = route_ids.shape
    capacity = 2 * tok_rows * per_token // n_ep
    model_width = w_down.shape[2]
    slot_count = experts * capacity
    pair_int = slot_assignment(route_ids, experts, capacity)
    token_selection = jnp.sum(
        pair_int.reshape(batches, tok_rows, per_token, slot_count), axis=2
    ).astype(jnp.bfloat16)
    pair_pick = pair_int.astype(jnp.bfloat16)
    complete_output = lax.all_gather(block_tokens, "tp", axis=2, tiled=True)
    outgoing = jnp.einsum(
        "pca,pcv->pav", token_selection, complete_output, preferred_element_type=jnp.float32
    ).astype(jnp.bfloat16)
    outgoing = outgoing.reshape(batches, experts, capacity, model_width)
    arrived = lax.all_to_all(outgoing, "ep", split_axis=1, concat_axis=1, tiled=True)
    arrived = arrived.reshape(batches, n_ep, local_count, capacity, model_width)
    gate_activated = jnp.einsum(
        "bslcd,ldf->bslcf", arrived, w_gate, preferred_element_type=jnp.float32
    )
    up_act = jnp.einsum("bslcd,ldf->bslcf", arrived, w_up, preferred_element_type=jnp.float32)
    hidden = (jax.nn.silu(gate_activated) * up_act).astype(jnp.bfloat16)
    partial_value = jnp.einsum(
        "bslcf,lfd->bslcd", hidden, w_down, preferred_element_type=jnp.float32
    )
    partial_value = partial_value.reshape(batches, experts, capacity, model_width)
    returned = lax.all_to_all(
        partial_value.astype(jnp.bfloat16), "ep", split_axis=1, concat_axis=1, tiled=True
    )
    pair_rows = jnp.einsum(
        "shz,szj->shj",
        pair_pick,
        returned.reshape(batches, slot_count, model_width),
        preferred_element_type=jnp.float32,
    )
    expert_out = lax.psum_scatter(
        pair_rows.astype(jnp.bfloat16), "tp", scatter_dimension=2, tiled=True
    )
    outputs = expert_out.reshape(batches, tok_rows, per_token, expert_out.shape[2]).astype(
        jnp.float32
    )
    return jnp.sum(routing_probability[:, :, :, None] * outputs, axis=2).astype(jnp.bfloat16)


def shards(tokens, routes, route_weight, w_gate, w_up, w_down):
    results = [
        moe_layer(
            tokens[batch_index : batch_index + 1],
            routes[batch_index : batch_index + 1],
            route_weight[batch_index : batch_index + 1],
            w_gate,
            w_up,
            w_down,
        )
        for batch_index in range(tokens.shape[0])
    ]
    return jnp.concatenate(results, axis=0)


def solution(mesh):
    return jax.shard_map(
        shards,
        mesh=mesh,
        in_specs=(
            P(None, "ep", "tp"),
            P(None, "ep", None),
            P(None, "ep", None),
            P("ep", None, "tp"),
            P("ep", None, "tp"),
            P("ep", "tp", None),
        ),
        out_specs=P(None, "ep", "tp"),
        check_vma=False,
    )
```

profile of v0, /device:TPU:1, one launch (start us, length us, event | category | flops | bytes accessed | tf_op | source)
XLA Modules:
  0.0 322.1 jit_solution(12448401226642420747)
XLA Ops:
  6.5 0.0 copy-start
  6.5 0.8 fusion.89
  7.3 0.1 copy.44
  7.4 0.1 reshape.580
  7.5 0.1 fusion.83
  7.6 0.2 reduce_window_sum.17
  7.8 0.2 select_reduce_fusion.1
  7.9 0.1 reduce_sum.59
  8.0 0.1 copy.45
  8.1 0.1 copy.51
  8.2 0.1 reshape.589
  8.3 0.1 fusion.79
  8.4 0.2 reduce_window_sum.18
  8.5 0.2 select_reduce_fusion
  8.7 0.1 reduce_sum.63
  8.8 0.1 copy.52
  8.9 0.7 bitcast_add_fusion.1
  9.6 0.1 copy.46
  9.7 0.1 convert_reduce_fusion.1
  9.8 0.7 fusion.88
  10.5 20.6 %all_gather.6 = bf16[1,16,4096]{2,1,0:T(8,128)(2,1)S(1)} all-gather(bf16[1,16,512]{2,1,0:T(8,128)(2,1)S(1)} %get-tuple-element.5), channel_id=1, replica_groups=mesh['ep'=64,'tp'=8] {'tp'}, dimensions={2}, use_global_device_ids=true | all-gather | bytes 147456 | tf_op jit(solution)/shard_map/all_gather | solution.py:34
  31.1 0.7 convolution_convert_fusion.3
  31.9 2.2 reshape.582
  34.1 20.4 %all-to-all-start = ((bf16[1,64,4,4096]{3,2,0,1:T(4,128)(2,1)}), bf16[1,64,4,4096]{3,2,0,1:T(4,128)(2,1)S(1)}, u32[]{:S(2)}, u32[]{:S(2)}) async-start(bf16[1,64,4,4096]{3,2,0,1:T(4,128)(2,1)} %bitcast.164), calls=%async_computation | async-start | bytes 4194304 | tf_op jit(solution)/shard_map/all_to_all | solution.py:39
  54.5 0.1 copy.53
  54.5 20.3 %all_gather.7 = bf16[1,16,4096]{2,1,0:T(8,128)(2,1)S(1)} all-gather(bf16[1,16,512]{2,1,0:T(8,128)(2,1)S(1)} %get-tuple-element.6), channel_id=1, replica_groups=mesh['ep'=64,'tp'=8] {'tp'}, dimensions={2}, use_global_device_ids=true | all-gather | bytes 147456 | tf_op jit(solution)/shard_map/all_gather | solution.py:34
  74.8 0.1 convert_reduce_fusion
  74.9 2.1 convolution_convert_fusion.2
  77.0 4.1 %reshape.591 = bf16[1,64,4,4096]{3,2,1,0:T(4,128)(2,1)} reshape(bf16[256,4096]{1,0:T(8,128)(2,1)} %convolution_convert_fusion.2) | data formatting | bytes 4194304 | tf_op jit(solution)/shard_map/reshape | solution.py:38
  81.1 24.6 %all-to-all-done = bf16[1,64,4,4096]{3,2,0,1:T(4,128)(2,1)S(1)} async-done(((bf16[1,64,4,4096]{3,2,0,1:T(4,128)(2,1)}), bf16[1,64,4,4096]{3,2,0,1:T(4,128)(2,1)S(1)}, u32[]{:S(2)}, u32[]{:S(2)}) %all-to-all-start) | async-done | bytes 2097184 | tf_op jit(solution)/shard_map/all_to_all | solution.py:39
  105.7 6.0 %all-to-all-start.2 = ((bf16[1,64,4,4096]{3,2,0,1:T(4,128)(2,1)}), bf16[1,64,4,4096]{3,2,0,1:T(4,128)(2,1)}, u32[]{:S(2)}, u32[]{:S(2)}) async-start(bf16[1,64,4,4096]{3,2,0,1:T(4,128)(2,1)} %bitcast.165), calls=%async_computation.3 | async-start | bytes 4194304 | tf_op jit(solution)/shard_map/all_to_all | solution.py:39
  111.7 3.7 %fusion.16 = f32[1,64,1,4,128]{4,1,3,0,2:T(8,128)S(1)} fusion(bf16[1,64,4,4096]{3,2,0,1:T(4,128)(2,1)S(1)} %all-to-all-done, bf16[1,4096,128]{2,1,0:T(8,128)(2,1)} %param.9), kind=kOutput, calls=%fused_computation.22 | convolution fusion | flops 268435456 | bytes 3276800 | tf_op jit(solution)/shard_map/bslcd,ldf->bslcf/dot_general | solution.py:41
  115.4 0.0 copy-done
  115.4 5.6 %fusion = bf16[1,64,4,4096]{3,1,2,0:T(8,128)(2,1)} fusion(bf16[1,128,4096]{2,1,0:T(8,128)(2,1)S(1)} %copy-done, bf16[1,64,4,4096]{3,2,0,1:T(4,128)(2,1)S(1)} %all-to-all-done, bf16[1,4096,128]{2,1,0:T(8,128)(2,1)} %param.10, f32[1,64,1,4,128]{4,1,3,0,2:T(8,128)S(1)} %fusion.16), kind=kOutput, calls=%fused_computation.4 | convolution fusion | flops 538116096 | bytes 6422528 | tf_op jit(solution)/shard_map/bslcf,lfd->bslcd/dot_general | solution.py:46
  121.1 4.5 %copy.49 = bf16[1,64,4,4096]{3,2,0,1:T(4,128)(2,1)} copy(bf16[1,64,4,4096]{3,1,2,0:T(8,128)(2,1)} %fusion) | data formatting | bytes 4194304 | tf_op jit(solution)/shard_map/convert_element_type | solution.py:51
  125.6 0.0 copy-start.2
  125.6 37.2 %all-to-all-done.2 = bf16[1,64,4,4096]{3,2,0,1:T(4,128)(2,1)} async-done(((bf16[1,64,4,4096]{3,2,0,1:T(4,128)(2,1)}), bf16[1,64,4,4096]{3,2,0,1:T(4,128)(2,1)}, u32[]{:S(2)}, u32[]{:S(2)}) %all-to-all-start.2) | async-done | bytes 2097184 | tf_op jit(solution)/shard_map/all_to_all | solution.py:39
  162.8 6.0 %all-to-all-start.1 = ((bf16[1,64,4,4096]{3,2,0,1:T(4,128)(2,1)}), bf16[1,64,4,4096]{3,2,0,1:T(4,128)(2,1)}, u32[]{:S(2)}, u32[]{:S(2)}) async-start(bf16[1,64,4,4096]{3,2,0,1:T(4,128)(2,1)} %copy.49), calls=%async_computation.1 | async-start | bytes 4194304 | tf_op jit(solution)/shard_map/all_to_all | solution.py:50
  168.9 0.0 copy-done.2
  168.9 4.1 %fusion.22 = f32[1,64,1,4,128]{4,1,3,0,2:T(8,128)S(1)} fusion(bf16[1,64,4,4096]{3,2,0,1:T(4,128)(2,1)} %all-to-all-done.2, bf16[1,4096,128]{2,1,0:T(8,128)(2,1)S(1)} %copy-done.2), kind=kOutput, calls=%fused_computation.24 | convolution fusion | flops 268435456 | bytes 3276800 | tf_op jit(solution)/shard_map/bslcd,ldf->bslcf/dot_general | solution.py:41
  173.0 4.9 %fusion.1 = bf16[1,64,4,4096]{3,1,2,0:T(8,128)(2,1)S(1)} fusion(bf16[1,128,4096]{2,1,0:T(8,128)(2,1)S(1)} %copy-done, bf16[1,64,4,4096]{3,2,0,1:T(4,128)(2,1)} %all-to-all-done.2, bf16[1,4096,128]{2,1,0:T(8,128)(2,1)} %param.10, f32[1,64,1,4,128]{4,1,3,0,2:T(8,128)S(1)} %fusion.22), kind=kOutput, calls=%fused_computation.5 | convolution fusion | flops 538116096 | bytes 6422528 | tf_op jit(solution)/shard_map/bslcf,lfd->bslcd/dot_general | solution.py:46
  177.9 3.0 copy.56
  180.8 39.1 %all-to-all-done.1 = bf16[1,64,4,4096]{3,2,0,1:T(4,128)(2,1)} async-done(((bf16[1,64,4,4096]{3,2,0,1:T(4,128)(2,1)}), bf16[1,64,4,4096]{3,2,0,1:T(4,128)(2,1)}, u32[]{:S(2)}, u32[]{:S(2)}) %all-to-all-start.1) | async-done | bytes 2097184 | tf_op jit(solution)/shard_map/all_to_all | solution.py:50
  220.0 5.8 %all-to-all-start.3 = ((bf16[1,64,4,4096]{3,2,0,1:T(4,128)(2,1)}), bf16[1,64,4,4096]{3,2,0,1:T(4,128)(2,1)S(1)}, u32[]{:S(2)}, u32[]{:S(2)}) async-start(bf16[1,64,4,4096]{3,2,0,1:T(4,128)(2,1)} %copy.56), calls=%async_computation.4 | async-start | bytes 4194304 | tf_op jit(solution)/shard_map/all_to_all | solution.py:50
  225.8 0.0 reduce-scatter.3.cloned.1.call-start
  225.9 4.0 %reshape.588 = bf16[256,4096]{1,0:T(8,128)(2,1)} reshape(bf16[1,64,4,4096]{3,2,0,1:T(4,128)(2,1)} %all-to-all-done.1) | data formatting | bytes 4194304 | tf_op jit(solution)/shard_map/reshape.32
  229.9 3.1 fusion.2
  232.9 0.0 reduce-scatter.3.cloned.1.call-update
  232.9 0.0 reduce-scatter.5.cloned.1.call-start
  233.0 44.0 %all-to-all-done.3 = bf16[1,64,4,4096]{3,2,0,1:T(4,128)(2,1)S(1)} async-done(((bf16[1,64,4,4096]{3,2,0,1:T(4,128)(2,1)}), bf16[1,64,4,4096]{3,2,0,1:T(4,128)(2,1)S(1)}, u32[]{:S(2)}, u32[]{:S(2)}) %all-to-all-start.3) | async-done | bytes 2097184 | tf_op jit(solution)/shard_map/all_to_all | solution.py:50
  277.0 2.1 reshape.594
  279.1 0.0 copy-start.1
  279.1 3.1 fusion.3
  282.2 0.0 reduce-scatter.5.cloned.1.call-update
  282.2 0.0 copy-done.1
  282.2 0.1 copy.43
  282.3 0.1 copy.50
  282.4 0.0 reduce-scatter.3.cloned.1.call-done
  282.4 1.1 fusion.61
  283.4 30.2 %reduce-scatter.5.cloned.1.call-done = bf16[1,128,512]{2,1,0:T(8,128)(2,1)} async-done(((bf16[1,128,4096]{2,1,0:T(8,128)(2,1)}), bf16[1,128,512]{2,1,0:T(8,128)(2,1)}) %reduce-scatter.5.cloned.1.call-update) | async-done | bytes 131088 | tf_op jit(solution)/shard_map/reduce_scatter | solution.py:59
  313.6 1.1 fusion.60
  314.7 0.6 pad_maximum_fusion
  (3 shorter events, 0.0 us)
Async XLA Ops:
  6.5 108.9 %copy-start = (bf16[1,128,4096]{2,1,0:T(8,128)(2,1)S(1)}, bf16[1,128,4096]{2,1,0:T(8,128)(2,1)}, u32[]{:S(2)}) copy-start(bf16[1,128,4096]{2,1,0:T(8,128)(2,1)} %param.11) | copy-start | bytes 3145732
  34.1 71.6 %all-to-all-start = ((bf16[1,64,4,4096]{3,2,0,1:T(4,128)(2,1)}), bf16[1,64,4,4096]{3,2,0,1:T(4,128)(2,1)S(1)}, u32[]{:S(2)}, u32[]{:S(2)}) async-start(bf16[1,64,4,4096]{3,2,0,1:T(4,128)(2,1)} %bitcast.164), calls=%async_computation | async-start | bytes 4194304 | tf_op jit(solution)/shard_map/all_to_all | solution.py:39
  105.7 57.1 %all-to-all-start.2 = ((bf16[1,64,4,4096]{3,2,0,1:T(4,128)(2,1)}), bf16[1,64,4,4096]{3,2,0,1:T(4,128)(2,1)}, u32[]{:S(2)}, u32[]{:S(2)}) async-start(bf16[1,64,4,4096]{3,2,0,1:T(4,128)(2,1)} %bitcast.165), calls=%async_computation.3 | async-start | bytes 4194304 | tf_op jit(solution)/shard_map/all_to_all | solution.py:39
  125.6 43.3 %copy-start.2 = (bf16[1,4096,128]{2,1,0:T(8,128)(2,1)S(1)}, bf16[1,4096,128]{2,1,0:T(8,128)(2,1)}, u32[]{:S(2)}) copy-start(bf16[1,4096,128]{2,1,0:T(8,128)(2,1)} %param.9) | copy-start | bytes 3145732
  162.8 57.1 %all-to-all-start.1 = ((bf16[1,64,4,4096]{3,2,0,1:T(4,128)(2,1)}), bf16[1,64,4,4096]{3,2,0,1:T(4,128)(2,1)}, u32[]{:S(2)}, u32[]{:S(2)}) async-start(bf16[1,64,4,4096]{3,2,0,1:T(4,128)(2,1)} %copy.49), calls=%async_computation.1 | async-start | bytes 4194304 | tf_op jit(solution)/shard_map/all_to_all | solution.py:50
  220.0 57.0 %all-to-all-start.3 = ((bf16[1,64,4,4096]{3,2,0,1:T(4,128)(2,1)}), bf16[1,64,4,4096]{3,2,0,1:T(4,128)(2,1)S(1)}, u32[]{:S(2)}, u32[]{:S(2)}) async-start(bf16[1,64,4,4096]{3,2,0,1:T(4,128)(2,1)} %copy.56), calls=%async_computation.4 | async-start | bytes 4194304 | tf_op jit(solution)/shard_map/all_to_all | solution.py:50
  225.8 56.5 %reduce-scatter.3.cloned.1.call-start = ((), (), s32[]{:S(2)}) async-start(), calls=%async_computation.6 | async-start | bytes 1179648 | tf_op jit(solution)/shard_map/reduce_scatter | solution.py:59
  232.9 80.7 %reduce-scatter.5.cloned.1.call-start = ((), (), s32[]{:S(2)}) async-start(), calls=%async_computation.7 | async-start | bytes 1179648 | tf_op jit(solution)/shard_map/reduce_scatter | solution.py:59
  279.1 3.1 copy-start.1
Sparse Core Ops, SparseCore 0:
  233.1 36.7 reduce-scatter.2
  282.3 31.2 reduce-scatter.4
where the time goes:
time: 327 us; the launch traced here: 322 us
  waiting for transfers between devices  175 us (54%)
  blocking collectives  40.9 us (13%)
  starting transfers between devices  38.4 us (12%)
  matrix products  27.2 us (8%)
  local copies, waits for them, and re-layouts  22.4 us (7%)
  between operations  13.6 us (4%)
  other arithmetic  4.54 us (1%)
    all_to_all x2, waiting for transfers between devices, moe_layer(): lax.all_to_all(partial_value.astype(jnp.bfloat16), 'ep', split_axis=1, co...  83.2 us
    all_to_all x2, waiting for transfers between devices, moe_layer(): lax.all_to_all(outgoing, 'ep', split_axis=1, concat_axis=1, tiled=True)  61.8 us
    all_gather x2, blocking collectives, moe_layer(): complete_output = lax.all_gather(block_tokens, 'tp', axis=2, tiled=True)  40.9 us
    reduce_scatter x2, waiting for transfers between devices, moe_layer(): lax.psum_scatter(pair_rows.astype(jnp.bfloat16), 'tp', scatter_dimension=...  30.2 us
    all_to_all x2, starting transfers between devices, moe_layer(): lax.all_to_all(outgoing, 'ep', split_axis=1, concat_axis=1, tiled=True)  26.4 us
    all_to_all x2, starting transfers between devices, moe_layer(): lax.all_to_all(partial_value.astype(jnp.bfloat16), 'ep', split_axis=1, co...  11.9 us
    dot_general x2, matrix products, moe_layer(): jnp.einsum('bslcf,lfd->bslcd', hidden, w_down, preferred_element_type=jnp...  10.5 us
    dot_general x2, matrix products, moe_layer(): jnp.einsum('bslcd,ldf->bslcf', arrived, w_gate, preferred_element_type=jn...  7.78 us
  transfers between devices with their start and end apart: 6, of which 5 were waited for; matrix products, arithmetic and copies ran while one was open for 14% of the time, Pallas kernels for 0%

commit v1 on v0

v1 whole, which is shorter than its diff:
```python
import functools

import jax
import jax.numpy as jnp
from jax import lax
from jax.experimental import pallas as pl
from jax.experimental.pallas import tpu as pltpu
from jax.sharding import PartitionSpec as P

MESH = pl.DeviceIdType.MESH
CHUNKS = 4
OFFSETS = (0, 0, 3, 3)


def log2(n):
    return n.bit_length() - 1


def kernel(
    n_ep, n_tp, batches, cap,
    routes_t, gains_t, tokens, w_gate, w_up, w_down, out,
    outgoing, gathered, combine, w_in, w_out, total, hidden,
    sum_right, sum_left, got_right, got_left, answer, returned,
    own_sem, w_sem, go_send, go_recv, ag_send, ag_recv,
    right_send, right_recv, left_send, left_recv, back_send, back_recv,
):
    me = lax.axis_index("ep")
    place = lax.axis_index("tp")
    right, left = lax.rem(place + 1, n_tp), lax.rem(place + n_tp - 1, n_tp)
    per = n_ep // CHUNKS
    group, seat = lax.div(me, per), lax.rem(me, per)
    top, toks = routes_t.shape
    rows = batches * cap
    slots = n_ep * rows
    features = tokens.shape[1]
    units = w_gate.shape[2]
    many = per * rows

    def reach(c):
        far = n_tp // 2
        near = n_tp - 1 - far
        return (far, near) if c % 2 == 0 else (near, far)

    weight_copies = [
        pltpu.make_async_copy(w_gate, w_in.at[:, :, pl.ds(0, units)], w_sem.at[0]),
        pltpu.make_async_copy(w_up, w_in.at[:, :, pl.ds(units, units)], w_sem.at[1]),
    ] + [
        pltpu.make_async_copy(
            w_down.at[:, pl.ds(g * features, features)], w_out.at[g], w_sem.at[2 + g]
        )
        for g in range(n_tp)
    ]
    for copy in weight_copies:
        copy.start()

    barrier = pltpu.get_barrier_semaphore()

    @pl.loop(1, n_ep)
    def _(i):
        pl.semaphore_signal(
            barrier, inc=1, device_id={"ep": lax.rem(me + i, n_ep)}, device_id_type=MESH
        )

    neighbours = (left, right) if n_tp > 2 else (right,)
    for neighbour in neighbours:
        pl.semaphore_signal(barrier, inc=1, device_id={"tp": neighbour}, device_id_type=MESH)

    slot = lax.broadcasted_iota(jnp.int32, (slots, toks), 0)
    token = lax.broadcasted_iota(jnp.int32, (slots, toks), 1)
    expert = slot >> log2(rows)
    hits = jnp.zeros((slots, toks), jnp.float32)
    gains = jnp.zeros((slots, toks), jnp.float32)
    for k in range(top):
        match = routes_t[k : k + 1, :] == expert
        hits += jnp.where(match, 1.0, 0.0)
        gains += jnp.where(match, gains_t[k : k + 1, :], 0.0)
    block = log2(toks // batches)
    first = lax.broadcasted_iota(jnp.int32, (toks, toks), 0)
    second = lax.broadcasted_iota(jnp.int32, (toks, toks), 1)
    earlier = jnp.where(
        (first < second) & ((first >> block) == (second >> block)), 1.0, 0.0
    ).astype(jnp.bfloat16)
    rank = jnp.dot(hits.astype(jnp.bfloat16), earlier, preferred_element_type=jnp.float32)
    wanted = (slot & (cap - 1)).astype(jnp.float32)
    same = ((slot & (rows - 1)) >> log2(cap)) == (token >> block)
    picked = jnp.where((rank == wanted) & same, hits, 0.0)
    combine[...] = picked * gains
    outgoing[...] = (
        jnp.dot(picked.astype(jnp.bfloat16), tokens[...], preferred_element_type=jnp.float32)
        .reshape(n_ep, rows, features)
        .astype(jnp.bfloat16)
    )

    pl.semaphore_wait(barrier, n_ep - 1 + len(neighbours))

    own_go = pltpu.make_async_copy(outgoing.at[me], gathered.at[0, 0, seat], own_sem.at[0])
    own_go.start()
    for c in range(CHUNKS):

        @pl.loop(1 if c == 0 else 0, per)
        def _(i):
            peer = lax.rem(group + c, CHUNKS) * per + lax.rem(seat + i, per)
            pltpu.make_async_remote_copy(
                src_ref=outgoing.at[peer],
                dst_ref=gathered.at[c, 0, seat],
                send_sem=go_send.at[c],
                recv_sem=go_recv.at[c],
                device_id={"ep": peer},
                device_id_type=MESH,
            ).start()

    def go_bytes(c):
        n = per - 1 if c == 0 else per
        if n == 0:
            return None
        return pltpu.make_async_remote_copy(
            src_ref=outgoing.at[pl.ds(0, n)],
            dst_ref=gathered.at[c, 0, pl.ds(0, n)],
            send_sem=go_send.at[c],
            recv_sem=go_recv.at[c],
            device_id={"tp": right},
            device_id_type=MESH,
        )

    def back_bytes(c):
        n = per - 1 if c == 0 else per
        if n == 0:
            return None
        return pltpu.make_async_remote_copy(
            src_ref=answer.at[c, pl.ds(0, n)],
            dst_ref=returned.at[pl.ds(0, n)],
            send_sem=back_send.at[c],
            recv_sem=back_recv.at[c],
            device_id={"tp": right},
            device_id_type=MESH,
        )

    def pass_on(c, source, slot_id, neighbour):
        return pltpu.make_async_remote_copy(
            src_ref=gathered.at[c, source],
            dst_ref=gathered.at[c, slot_id],
            send_sem=ag_send.at[c, slot_id],
            recv_sem=ag_recv.at[c, slot_id],
            device_id={"tp": neighbour},
            device_id_type=MESH,
        )

    def multiply(c, slot_id, origin):
        value = gathered[c, slot_id].astype(jnp.float32).reshape(many, features)
        return jnp.dot(
            value.astype(jnp.bfloat16), w_in[origin], preferred_element_type=jnp.float32
        )

    gather_copies, ring_copies = [], []

    def gather_begin(c):
        to_right, to_left = reach(c)
        if c == 0:
            own_go.wait()
        arrived = go_bytes(c)
        if arrived is not None:
            arrived.wait_recv()
        for length, slot_id, neighbour in ((to_right, 1, right), (to_left, to_right + 1, left)):
            if length > 0:
                copy = pass_on(c, 0, slot_id, neighbour)
                copy.start()
                gather_copies.append(copy)
        if c == 0:
            weight_copies[0].wait()
            weight_copies[1].wait()
        total[c] = multiply(c, 0, place)

    def gather_hop(c, j):
        to_right, to_left = reach(c)
        todo = []
        for length, base, neighbour, step in (
            (to_right, 0, right, n_tp - j),
            (to_left, to_right, left, j),
        ):
            if j <= length:
                pass_on(c, 0, base + j, neighbour).wait_recv()
                if j < length:
                    copy = pass_on(c, base + j, base + j + 1, neighbour)
                    copy.start()
                    gather_copies.append(copy)
                todo.append((base + j, lax.rem(place + step, n_tp)))
        for slot_id, origin in todo:
            total[c] += multiply(c, slot_id, origin)

    def activate(c):
        gate, up = total[c, :, :units], total[c, :, units:]
        hidden[c] = (gate / (1.0 + jnp.exp(-gate)) * up).astype(jnp.bfloat16)

    def part(c, target):
        return jnp.dot(hidden[c], w_out[target], preferred_element_type=jnp.float32)

    def ring(c, j, to_right):
        sums, got, send, recv, neighbour = (
            (sum_right, got_right, right_send, right_recv, right)
            if to_right
            else (sum_left, got_left, left_send, left_recv, left)
        )
        return pltpu.make_async_remote_copy(
            src_ref=sums.at[c, j],
            dst_ref=got.at[c, j],
            send_sem=send.at[c, j],
            recv_sem=recv.at[c, j],
            device_id={"tp": neighbour},
            device_id_type=MESH,
        )

    def reduce_step(c, j):
        if j == 0:
            if c == 0:
                for copy in weight_copies[2:]:
                    copy.wait()
            activate(c)
        for length, to_right in zip(reach(c), (True, False)):
            if j < length:
                ahead = length - j if to_right else n_tp - (length - j)
                value = part(c, lax.rem(place + ahead, n_tp))
                sums, got = (sum_right, got_right) if to_right else (sum_left, got_left)
                if j > 0:
                    ring(c, j - 1, to_right).wait_recv()
                    value += got[c, j - 1].astype(jnp.float32)
                sums[c, j] = value.astype(jnp.bfloat16)
                copy = ring(c, j, to_right)
                copy.start()
                ring_copies.append(copy)

    own_back = pltpu.make_async_copy(answer.at[0, seat], returned.at[me], own_sem.at[1])

    def reduce_end(c):
        value = part(c, place)
        for length, to_right in zip(reach(c), (True, False)):
            if length > 0:
                ring(c, length - 1, to_right).wait_recv()
                got = got_right if to_right else got_left
                value += got[c, length - 1].astype(jnp.float32)
        answer[c] = value.reshape(per, rows, features).astype(jnp.bfloat16)
        if c == 0:
            own_back.start()

        @pl.loop(1 if c == 0 else 0, per)
        def _(i):
            other = lax.rem(seat + i, per)
            peer = lax.rem(group + CHUNKS - c, CHUNKS) * per + other
            pltpu.make_async_remote_copy(
                src_ref=answer.at[c, other],
                dst_ref=returned.at[me],
                send_sem=back_send.at[c],
                recv_sem=back_recv.at[c],
                device_id={"ep": peer},
                device_id_type=MESH,
            ).start()

    hops = n_tp // 2
    events = []
    for c in range(CHUNKS):
        start = OFFSETS[c]
        events.append((start, c, functools.partial(gather_begin, c)))
        for j in range(1, hops + 1):
            events.append((start + j, c, functools.partial(gather_hop, c, j)))
        for j in range(hops):
            events.append((start + hops + 1 + j, c, functools.partial(reduce_step, c, j)))
        events.append((start + 2 * hops + 1, c, functools.partial(reduce_end, c)))
    for _, _, run in sorted(events, key=lambda event: event[:2]):
        run()

    own_back.wait()
    for c in range(CHUNKS):
        arrived = back_bytes(c)
        if arrived is not None:
            arrived.wait_recv()
    values = returned[...].astype(jnp.float32).reshape(slots, features).astype(jnp.bfloat16)
    weights = combine[...]
    high = weights.astype(jnp.bfloat16)
    low = (weights - high.astype(jnp.float32)).astype(jnp.bfloat16)
    over_slots = (((0,), (0,)), ((), ()))
    mixed = lax.dot_general(high, values, over_slots, preferred_element_type=jnp.float32)
    mixed += lax.dot_general(low, values, over_slots, preferred_element_type=jnp.float32)
    out[...] = mixed.astype(jnp.bfloat16)

    for c in range(CHUNKS):
        for sent in (go_bytes(c), back_bytes(c)):
            if sent is not None:
                sent.wait_send()
    for copy in gather_copies + ring_copies:
        copy.wait_send()


def shards(tokens, routes, route_weight, w_gate, w_up, w_down):
    n_ep, n_tp = lax.axis_size("ep"), lax.axis_size("tp")
    batches, tok_rows, features = tokens.shape
    top = routes.shape[2]
    cap = 2 * tok_rows * top // n_ep
    toks, rows = batches * tok_rows, batches * cap
    units = w_gate.shape[2]
    per = n_ep // CHUNKS
    many = per * rows
    hops = n_tp // 2
    dma = pltpu.SemaphoreType.DMA
    vmem = pl.BlockSpec(memory_space=pltpu.VMEM)
    hbm = pl.BlockSpec(memory_space=pl.ANY)
    bf16, f32 = jnp.bfloat16, jnp.float32
    ring = pltpu.VMEM((CHUNKS, hops, many, features), bf16)
    out = pl.pallas_call(
        functools.partial(kernel, n_ep, n_tp, batches, cap),
        out_shape=jax.ShapeDtypeStruct((toks, features), bf16),
        in_specs=[vmem, vmem, vmem, hbm, hbm, hbm],
        out_specs=vmem,
        scratch_shapes=[
            pltpu.VMEM((n_ep, rows, features), bf16),
            pltpu.VMEM((CHUNKS, n_tp, per, rows, features), bf16),
            pltpu.VMEM((n_ep * rows, toks), f32),
            pltpu.VMEM((n_tp, features, 2 * units), bf16),
            pltpu.VMEM((n_tp, units, features), bf16),
            pltpu.VMEM((CHUNKS, many, 2 * units), f32),
            pltpu.VMEM((CHUNKS, many, units), bf16),
            ring,
            ring,
            ring,
            ring,
            pltpu.VMEM((CHUNKS, per, rows, features), bf16),
            pltpu.VMEM((n_ep, rows, features), bf16),
            dma((2,)),
            dma((2 + n_tp,)),
            dma((CHUNKS,)),
            dma((CHUNKS,)),
            dma((CHUNKS, n_tp)),
            dma((CHUNKS, n_tp)),
            dma((CHUNKS, hops)),
            dma((CHUNKS, hops)),
            dma((CHUNKS, hops)),
            dma((CHUNKS, hops)),
            dma((CHUNKS,)),
            dma((CHUNKS,)),
        ],
        compiler_params=pltpu.CompilerParams(
            collective_id=0, has_side_effects=True, vmem_limit_bytes=48 * 1024 * 1024
        ),
        name="expert_layer",
    )(
        routes.reshape(toks, top).T,
        route_weight.reshape(toks, top).T,
        tokens.reshape(toks, features),
        w_gate.reshape(n_tp, features, units),
        w_up.reshape(n_tp, features, units),
        w_down.reshape(units, n_tp * features),
    )
    return out.reshape(batches, tok_rows, features)


def solution(mesh):
    return jax.shard_map(
        shards,
        mesh=mesh,
        in_specs=(
            P(None, "ep", "tp"),
            P(None, "ep", None),
            P(None, "ep", None),
            P("ep", None, "tp"),
            P("ep", None, "tp"),
            P("ep", "tp", None),
        ),
        out_specs=P(None, "ep", "tp"),
        check_vma=False,
    )
```

time: 327 us -> 125 us (0.38); the launches traced: 322 us -> 124 us
  waiting for transfers between devices: 175 us -> 0 us
  Pallas kernels: 0 us -> 119 us
  blocking collectives: 40.9 us -> 0 us
  starting transfers between devices: 38.4 us -> 0 us
  matrix products: 27.2 us -> 0 us
  local copies, waits for them, and re-layouts: 22.4 us -> 5.18 us
  between operations: 13.6 us -> 0.02 us
  other arithmetic: 4.54 us -> 0 us
    all_to_all x4 -> x0, waiting for transfers between devices: 145 us -> none  [the longest x2 83.2 us: moe_layer(): lax.all_to_all(partial_value.astype(jnp.bfloat16), 'ep', split_axis=1, co...]
    pallas_call x0 -> x1, Pallas kernels: none -> 119 us  [shards(): pl.pallas_call(functools.partial(kernel, n_ep, n_tp, batches, cap), out_s...]
    all_gather x2 -> x0, blocking collectives: 40.9 us -> none  [moe_layer(): complete_output = lax.all_gather(block_tokens, 'tp', axis=2, tiled=True)]
    all_to_all x4 -> x0, starting transfers between devices: 38.3 us -> none  [the longest x2 26.4 us: moe_layer(): lax.all_to_all(outgoing, 'ep', split_axis=1, concat_axis=1, tiled=True)]
    reduce_scatter x2 -> x0, waiting for transfers between devices: 30.2 us -> none  [moe_layer(): lax.psum_scatter(pair_rows.astype(jnp.bfloat16), 'tp', scatter_dimension=...]
    dot_general x8 -> x0, matrix products: 27.2 us -> none  [the longest x2 10.5 us: moe_layer(): jnp.einsum('bslcf,lfd->bslcd', hidden, w_down, preferred_element_type=jnp...]
    convert_element_type x2 -> x0, local copies, waits for them, and re-layouts: 7.51 us -> none  [moe_layer(): partial_value.astype(jnp.bfloat16)]
    reshape x4 -> x2, local copies, waits for them, and re-layouts: 6.53 us -> 0.16 us  [the longest x1 0.08 us: shards(): route_weight.reshape(toks, top)]
  transfers between devices with their start and end apart: 6 -> 0, of which waited for: 5 -> 0; matrix products, arithmetic and copies ran while one was open for 14% -> 0% of each run, Pallas kernels for 0% -> 0%
where the time goes in v1:
time: 125 us; the launch traced here: 124 us
  Pallas kernels  119 us (95%)
  local copies, waits for them, and re-layouts  5.18 us (4%)
    pallas_call x1, Pallas kernels, shards(): pl.pallas_call(functools.partial(kernel, n_ep, n_tp, batches, cap), out_s...  119 us
    unnamed x13, local copies, waits for them, and re-layouts  5.02 us

profile of v1, /device:TPU:1, one launch (start us, length us, event | category | flops | bytes accessed | tf_op | source)
XLA Modules:
  0.0 124.4 jit_solution(11515990944594004354)
XLA Ops:
  0.0 0.0 copy-start.4
  0.0 0.0 copy-start.3
  0.0 0.7 copy.7
  0.7 0.1 reshape.21
  0.8 0.0 copy-done.4
  0.8 0.1 reshape.22
  0.9 0.0 copy-done.3
  0.9 0.0 copy-start
  0.9 1.2 copy-done
  2.1 0.0 copy-start.1
  2.1 1.2 copy-done.1
  3.3 0.0 copy-start.2
  3.4 1.2 copy-done.2
  4.6 119.2 %expert_layer.1 = bf16[32,512]{1,0:T(8,128)(2,1)S(1)} custom-call(s32[8,32]{1,0:T(8,128)S(1)} %bitcast.16, f32[8,32]{1,0:T(8,128)S(1)} %bitcast.17, bf16[32,512]{1,0:T(8,128)(2,1)S(1)} %bitcast.15, bf16[8,512,128]{2,1,0:T(8,128)(2,1)S(1)} %bitcast.11, bf16[8,512,128]{2,1,0:T(8,128)(2,1)S(1)} %bitcast.12, bf16[128,4096]{1,0:T(8,128)(2,1)S(1)} %bitcast.13), custom_call_target="tpu_custom_call" | custom-call | tf_op jit(solution)/shard_map/expert_layer/pallas_call | solution.py:307
  123.8 0.6 copy.10
  (1 shorter events, 0.0 us)
Async XLA Ops:
  0.0 0.8 copy-start.4
  0.0 0.9 copy-start.3
  0.9 1.2 copy-start
  2.1 1.2 copy-start.1
  3.3 1.2 copy-start.2

commit v2 on v1

v2 whole, which is shorter than its diff:
```python
import functools

import jax
import jax.numpy as jnp
from jax import lax
from jax.experimental import pallas as pl
from jax.experimental.pallas import tpu as pltpu
from jax.sharding import PartitionSpec as P

MESH = pl.DeviceIdType.MESH
CHUNKS = 4
OFFSETS = (0, 1, 2, 3)
FAR_AT = 0.5


def log2(n):
    return n.bit_length() - 1


def kernel(
    n_ep, n_tp, batches, cap,
    routes_in, gains_in, tokens_in, w_gate, w_up, w_down, out,
    routes, weights, tokens, outgoing, gathered, combine, w_in, w_out, total, hidden,
    sum_right, sum_left, got_right, got_left, answer, returned,
    far_tokens, far_outgoing, far_answer, far_returned, far_mixed, far_got,
    in_sem, own_sem, w_sem, go_send, go_recv, ag_send, ag_recv,
    right_send, right_recv, left_send, left_recv, back_send, back_recv,
    far_send, far_recv, far_go_send, far_go_recv, far_back_send, far_back_recv,
):
    me = lax.axis_index("ep")
    place = lax.axis_index("tp")
    right, left = lax.rem(place + 1, n_tp), lax.rem(place + n_tp - 1, n_tp)
    opposite = lax.rem(place + n_tp // 2, n_tp)
    hops = n_tp // 2 - 1
    per = n_ep // CHUNKS
    group, seat = lax.div(me, per), lax.rem(me, per)
    top, toks = routes.shape[1], tokens.shape[0]
    rows = batches * cap
    slots = n_ep * rows
    features = tokens.shape[1]
    units = w_gate.shape[2]
    many = per * rows

    small_copies = [
        pltpu.make_async_copy(source, target, in_sem.at[i])
        for i, (source, target) in enumerate(
            ((routes_in, routes), (gains_in, weights), (tokens_in, tokens))
        )
    ]
    for copy in small_copies:
        copy.start()

    weight_copies = [
        pltpu.make_async_copy(w_gate, w_in.at[:, :, pl.ds(0, units)], w_sem.at[0]),
        pltpu.make_async_copy(w_up, w_in.at[:, :, pl.ds(units, units)], w_sem.at[1]),
    ] + [
        pltpu.make_async_copy(
            w_down.at[:, pl.ds(g * features, features)], w_out.at[g], w_sem.at[2 + g]
        )
        for g in range(n_tp)
    ]
    for copy in weight_copies:
        copy.start()

    barrier = pltpu.get_barrier_semaphore()

    @pl.loop(1, n_ep)
    def _(i):
        pl.semaphore_signal(
            barrier, inc=1, device_id={"ep": lax.rem(me + i, n_ep)}, device_id_type=MESH
        )

    neighbours = (left, right, opposite)
    for neighbour in neighbours:
        pl.semaphore_signal(barrier, inc=1, device_id={"tp": neighbour}, device_id_type=MESH)

    for copy in small_copies:
        copy.wait()
    token = lax.broadcasted_iota(jnp.int32, (toks, slots), 0)
    slot = lax.broadcasted_iota(jnp.int32, (toks, slots), 1)
    expert = slot >> log2(rows)
    hits = jnp.zeros((toks, slots), jnp.float32)
    gains = jnp.zeros((toks, slots), jnp.float32)
    chosen = jnp.concatenate([routes[b].T for b in range(batches)], axis=0)
    factor = jnp.concatenate([weights[b].T for b in range(batches)], axis=0)
    for k in range(top):
        match = chosen[:, k : k + 1] == expert
        hits += jnp.where(match, 1.0, 0.0)
        gains += jnp.where(match, factor[:, k : k + 1], 0.0)
    block = log2(toks // batches)
    first = lax.broadcasted_iota(jnp.int32, (toks, toks), 0)
    second = lax.broadcasted_iota(jnp.int32, (toks, toks), 1)
    earlier = jnp.where(
        (second < first) & ((first >> block) == (second >> block)), 1.0, 0.0
    ).astype(jnp.bfloat16)
    rank = jnp.dot(earlier, hits.astype(jnp.bfloat16), preferred_element_type=jnp.float32)
    wanted = (slot & (cap - 1)).astype(jnp.float32)
    same = ((slot & (rows - 1)) >> log2(cap)) == (token >> block)
    picked = jnp.where((rank == wanted) & same, hits, 0.0)
    combine[...] = picked * gains
    def place_tokens(source, target):
        rows_out = lax.dot_general(
            picked.astype(jnp.bfloat16),
            source[...],
            (((0,), (0,)), ((), ())),
            preferred_element_type=jnp.float32,
        )
        target[...] = rows_out.reshape(n_ep, rows, features).astype(jnp.bfloat16)

    place_tokens(tokens, outgoing)

    pl.semaphore_wait(barrier, n_ep - 1 + len(neighbours))

    def far_copy(source, target, i):
        return pltpu.make_async_remote_copy(
            src_ref=source,
            dst_ref=target,
            send_sem=far_send.at[i],
            recv_sem=far_recv.at[i],
            device_id={"tp": opposite},
            device_id_type=MESH,
        )

    token_swap = far_copy(tokens, far_tokens, 0)
    token_swap.start()

    def go(source, slot_id, own, send, recv):
        own.start()
        for c in range(CHUNKS):

            @pl.loop(1 if c == 0 else 0, per)
            def _(i):
                peer = lax.rem(group + c, CHUNKS) * per + lax.rem(seat + i, per)
                pltpu.make_async_remote_copy(
                    src_ref=source.at[peer],
                    dst_ref=gathered.at[c, slot_id, seat],
                    send_sem=send.at[c],
                    recv_sem=recv.at[c],
                    device_id={"ep": peer},
                    device_id_type=MESH,
                ).start()

    own_go = pltpu.make_async_copy(outgoing.at[me], gathered.at[0, 0, seat], own_sem.at[0])
    go(outgoing, 0, own_go, go_send, go_recv)
    far_slot = n_tp - 1
    own_far_go = pltpu.make_async_copy(
        far_outgoing.at[me], gathered.at[0, far_slot, seat], own_sem.at[2]
    )

    def far_dispatch():
        token_swap.wait_recv()
        place_tokens(far_tokens, far_outgoing)
        go(far_outgoing, far_slot, own_far_go, far_go_send, far_go_recv)

    def all_bytes(c, source, target, send, recv):
        n = per - 1 if c == 0 else per
        if n == 0:
            return None
        return pltpu.make_async_remote_copy(
            src_ref=source.at[pl.ds(0, n)],
            dst_ref=target.at[pl.ds(0, n)],
            send_sem=send.at[c],
            recv_sem=recv.at[c],
            device_id={"tp": right},
            device_id_type=MESH,
        )

    def go_bytes(c):
        return all_bytes(c, outgoing, gathered.at[c, 0], go_send, go_recv)

    def far_go_bytes(c):
        return all_bytes(c, far_outgoing, gathered.at[c, far_slot], far_go_send, far_go_recv)

    def back_bytes(c):
        return all_bytes(c, answer.at[c], returned, back_send, back_recv)

    def far_back_bytes(c):
        return all_bytes(c, far_answer.at[c], far_returned, far_back_send, far_back_recv)

    def pass_on(c, source, slot_id, neighbour):
        return pltpu.make_async_remote_copy(
            src_ref=gathered.at[c, source],
            dst_ref=gathered.at[c, slot_id],
            send_sem=ag_send.at[c, slot_id],
            recv_sem=ag_recv.at[c, slot_id],
            device_id={"tp": neighbour},
            device_id_type=MESH,
        )

    def multiply(c, slot_id, origin):
        value = gathered[c, slot_id].astype(jnp.float32).reshape(many, features)
        return jnp.dot(
            value.astype(jnp.bfloat16), w_in[origin], preferred_element_type=jnp.float32
        )

    gather_copies, ring_copies = [], []

    def gather_begin(c):
        to_right, to_left = hops, hops
        if c == 0:
            own_go.wait()
        arrived = go_bytes(c)
        if arrived is not None:
            arrived.wait_recv()
        for length, slot_id, neighbour in ((to_right, 1, right), (to_left, to_right + 1, left)):
            if length > 0:
                copy = pass_on(c, 0, slot_id, neighbour)
                copy.start()
                gather_copies.append(copy)
        if c == 0:
            weight_copies[0].wait()
            weight_copies[1].wait()
        total[c] = multiply(c, 0, place)

    def gather_hop(c, j):
        to_right, to_left = hops, hops
        todo = []
        for length, base, neighbour, step in (
            (to_right, 0, right, n_tp - j),
            (to_left, to_right, left, j),
        ):
            if j <= length:
                pass_on(c, 0, base + j, neighbour).wait_recv()
                if j < length:
                    copy = pass_on(c, base + j, base + j + 1, neighbour)
                    copy.start()
                    gather_copies.append(copy)
                todo.append((base + j, lax.rem(place + step, n_tp)))
        for slot_id, origin in todo:
            total[c] += multiply(c, slot_id, origin)

    def far_gather(c):
        if c == 0:
            own_far_go.wait()
        arrived = far_go_bytes(c)
        if arrived is not None:
            arrived.wait_recv()
        total[c] += multiply(c, far_slot, opposite)

    def activate(c):
        gate, up = total[c, :, :units], total[c, :, units:]
        hidden[c] = (gate / (1.0 + jnp.exp(-gate)) * up).astype(jnp.bfloat16)

    def part(c, target):
        return jnp.dot(hidden[c], w_out[target], preferred_element_type=jnp.float32)

    def ring(c, j, to_right):
        sums, got, send, recv, neighbour = (
            (sum_right, got_right, right_send, right_recv, right)
            if to_right
            else (sum_left, got_left, left_send, left_recv, left)
        )
        return pltpu.make_async_remote_copy(
            src_ref=sums.at[c, j],
            dst_ref=got.at[c, j],
            send_sem=send.at[c, j],
            recv_sem=recv.at[c, j],
            device_id={"tp": neighbour},
            device_id_type=MESH,
        )

    def reduce_step(c, j):
        if j == 0:
            if c == 0:
                for copy in weight_copies[2:]:
                    copy.wait()
            activate(c)
        for length, to_right in ((hops, True), (hops, False)):
            if j < length:
                ahead = length - j if to_right else n_tp - (length - j)
                value = part(c, lax.rem(place + ahead, n_tp))
                sums, got = (sum_right, got_right) if to_right else (sum_left, got_left)
                if j > 0:
                    ring(c, j - 1, to_right).wait_recv()
                    value += got[c, j - 1].astype(jnp.float32)
                sums[c, j] = value.astype(jnp.bfloat16)
                copy = ring(c, j, to_right)
                copy.start()
                ring_copies.append(copy)

    def back(c, source, target, own, send, recv):
        if c == 0:
            own.start()

        @pl.loop(1 if c == 0 else 0, per)
        def _(i):
            other = lax.rem(seat + i, per)
            peer = lax.rem(group + CHUNKS - c, CHUNKS) * per + other
            pltpu.make_async_remote_copy(
                src_ref=source.at[c, other],
                dst_ref=target.at[me],
                send_sem=send.at[c],
                recv_sem=recv.at[c],
                device_id={"ep": peer},
                device_id_type=MESH,
            ).start()

    own_back = pltpu.make_async_copy(answer.at[0, seat], returned.at[me], own_sem.at[1])
    own_far_back = pltpu.make_async_copy(
        far_answer.at[0, seat], far_returned.at[me], own_sem.at[3]
    )

    def far_reduce(c):
        value = part(c, opposite)
        far_answer[c] = value.reshape(per, rows, features).astype(jnp.bfloat16)
        back(c, far_answer, far_returned, own_far_back, far_back_send, far_back_recv)

    def reduce_end(c):
        value = part(c, place)
        for length, to_right in ((hops, True), (hops, False)):
            if length > 0:
                ring(c, length - 1, to_right).wait_recv()
                got = got_right if to_right else got_left
                value += got[c, length - 1].astype(jnp.float32)
        answer[c] = value.reshape(per, rows, features).astype(jnp.bfloat16)
        back(c, answer, returned, own_back, back_send, back_recv)

    events = [(FAR_AT, -1, far_dispatch)]
    for c in range(CHUNKS):
        start = OFFSETS[c]
        events.append((start, c, functools.partial(gather_begin, c)))
        for j in range(1, hops + 1):
            events.append((start + j, c, functools.partial(gather_hop, c, j)))
        events.append((start + hops, c, functools.partial(far_gather, c)))
        start += hops + 1
        for j in range(hops):
            events.append((start + j, c, functools.partial(reduce_step, c, j)))
        events.append((start, c, functools.partial(far_reduce, c)))
        events.append((start + hops, c, functools.partial(reduce_end, c)))
    for _, _, run in sorted(events, key=lambda event: event[:2]):
        run()

    scale = combine[...]
    high = scale.astype(jnp.bfloat16)
    low = (scale - high.astype(jnp.float32)).astype(jnp.bfloat16)

    def mix(source, own, arrivals):
        own.wait()
        for c in range(CHUNKS):
            arrived = arrivals(c)
            if arrived is not None:
                arrived.wait_recv()
        values = source[...].astype(jnp.float32).reshape(slots, features).astype(jnp.bfloat16)
        mixed = jnp.dot(high, values, preferred_element_type=jnp.float32)
        return mixed + jnp.dot(low, values, preferred_element_type=jnp.float32)

    far_mixed[...] = mix(far_returned, own_far_back, far_back_bytes)
    mixed_swap = far_copy(far_mixed, far_got, 1)
    mixed_swap.start()
    mixed = mix(returned, own_back, back_bytes)
    mixed_swap.wait_recv()
    out[...] = (mixed + far_got[...]).astype(jnp.bfloat16)

    for c in range(CHUNKS):
        for sent in (go_bytes(c), far_go_bytes(c), back_bytes(c), far_back_bytes(c)):
            if sent is not None:
                sent.wait_send()
    for copy in gather_copies + ring_copies + [token_swap, mixed_swap]:
        copy.wait_send()


def shards(tokens, routes, route_weight, w_gate, w_up, w_down):
    n_ep, n_tp = lax.axis_size("ep"), lax.axis_size("tp")
    batches, tok_rows, features = tokens.shape
    top = routes.shape[2]
    cap = 2 * tok_rows * top // n_ep
    toks, rows = batches * tok_rows, batches * cap
    units = w_gate.shape[2]
    per = n_ep // CHUNKS
    many = per * rows
    hops = n_tp // 2 - 1
    dma = pltpu.SemaphoreType.DMA
    vmem = pl.BlockSpec(memory_space=pltpu.VMEM)
    hbm = pl.BlockSpec(memory_space=pltpu.HBM)
    bf16, f32 = jnp.bfloat16, jnp.float32
    ring = pltpu.VMEM((CHUNKS, hops, many, features), bf16)
    out = pl.pallas_call(
        functools.partial(kernel, n_ep, n_tp, batches, cap),
        out_shape=jax.ShapeDtypeStruct((toks, features), bf16),
        in_specs=[hbm] * 6,
        out_specs=vmem,
        scratch_shapes=[
            pltpu.VMEM((batches, top, tok_rows), jnp.int32),
            pltpu.VMEM((batches, top, tok_rows), f32),
            pltpu.VMEM((toks, features), bf16),
            pltpu.VMEM((n_ep, rows, features), bf16),
            pltpu.VMEM((CHUNKS, n_tp, per, rows, features), bf16),
            pltpu.VMEM((toks, n_ep * rows), f32),
            pltpu.VMEM((n_tp, features, 2 * units), bf16),
            pltpu.VMEM((n_tp, units, features), bf16),
            pltpu.VMEM((CHUNKS, many, 2 * units), f32),
            pltpu.VMEM((CHUNKS, many, units), bf16),
            ring,
            ring,
            ring,
            ring,
            pltpu.VMEM((CHUNKS, per, rows, features), bf16),
            pltpu.VMEM((n_ep, rows, features), bf16),
            pltpu.VMEM((toks, features), bf16),
            pltpu.VMEM((n_ep, rows, features), bf16),
            pltpu.VMEM((CHUNKS, per, rows, features), bf16),
            pltpu.VMEM((n_ep, rows, features), bf16),
            pltpu.VMEM((toks, features), f32),
            pltpu.VMEM((toks, features), f32),
            dma((3,)),
            dma((4,)),
            dma((2 + n_tp,)),
            dma((CHUNKS,)),
            dma((CHUNKS,)),
            dma((CHUNKS, n_tp)),
            dma((CHUNKS, n_tp)),
            dma((CHUNKS, hops)),
            dma((CHUNKS, hops)),
            dma((CHUNKS, hops)),
            dma((CHUNKS, hops)),
            dma((CHUNKS,)),
            dma((CHUNKS,)),
            dma((2,)),
            dma((2,)),
            dma((CHUNKS,)),
            dma((CHUNKS,)),
            dma((CHUNKS,)),
            dma((CHUNKS,)),
        ],
        compiler_params=pltpu.CompilerParams(
            collective_id=0, has_side_effects=True, vmem_limit_bytes=67_043_328
        ),
        name="expert_layer",
    )(
        routes.swapaxes(1, 2),
        route_weight.swapaxes(1, 2),
        tokens.reshape(toks, features),
        w_gate.reshape(n_tp, features, units),
        w_up.reshape(n_tp, features, units),
        w_down.reshape(units, n_tp * features),
    )
    return out.reshape(batches, tok_rows, features)


def solution(mesh):
    return jax.shard_map(
        shards,
        mesh=mesh,
        in_specs=(
            P(None, "ep", "tp"),
            P(None, "ep", None),
            P(None, "ep", None),
            P("ep", None, "tp"),
            P("ep", None, "tp"),
            P("ep", "tp", None),
        ),
        out_specs=P(None, "ep", "tp"),
        check_vma=False,
    )
```

time: 125 us -> 107 us (0.86)
  Pallas kernels: 119 us -> 106 us
  local copies, waits for them, and re-layouts: 5.18 us -> 1.38 us
    pallas_call x1, Pallas kernels: 119 us -> 106 us  [shards(): pl.pallas_call(functools.partial(kernel, n_ep, n_tp, batches, cap), out_s...]
    unnamed x13 -> x1, local copies, waits for them, and re-layouts: 5.02 us -> 1.38 us
where the time goes in v2:
time: 107 us
  Pallas kernels  106 us (99%)
  local copies, waits for them, and re-layouts  1.38 us (1%)
    pallas_call x1, Pallas kernels, shards(): pl.pallas_call(functools.partial(kernel, n_ep, n_tp, batches, cap), out_s...  106 us

profile of v2, /device:TPU:1, one launch (start us, length us, event | category | flops | bytes accessed | tf_op | source)
XLA Modules:
  0.0 107.1 jit_solution(16516995087317083135)
XLA Ops:
  0.0 105.7 %expert_layer.1 = bf16[32,512]{1,0:T(8,128)(2,1)} custom-call(s32[2,8,16]{2,1,0:T(8,128)} %bitcast.12, f32[2,8,16]{2,1,0:T(8,128)} %bitcast.13, bf16[32,512]{1,0:T(8,128)(2,1)} %bitcast.11, bf16[8,512,128]{2,1,0:T(8,128)(2,1)} %bitcast.7, bf16[8,512,128]{2,1,0:T(8,128)(2,1)} %bitcast.8, bf16[128,4096]{1,0:T(8,128)(2,1)} %bitcast.9), custom_call_target="tpu_custom_call" | custom-call | tf_op jit(solution)/shard_map/expert_layer/pallas_call | solution.py:377
  105.7 1.4 %copy.8 = bf16[2,16,512]{2,1,0:T(8,128)(2,1)} copy(bf16[2,16,512]{2,1,0:T(8,128)(2,1)} %bitcast.10) | data formatting | bytes 65536

commit v3 on v2

--- a/solution.py
+++ b/solution.py
@@ -8,9 +8,12 @@
 from jax.sharding import PartitionSpec as P
 
 MESH = pl.DeviceIdType.MESH
-CHUNKS = 4
-OFFSETS = (0, 1, 2, 3)
-FAR_AT = 0.5
+DISTANCES = ((0,), (1,), (4,), (-3,), (3,), (-2,), (2,), (-1,))
+DEPTH = 8
+CORES = 2
+CHUNKS = len(DISTANCES)
+OFFSETS = (0, 0.5, 1, 1.5, 2, 2.5, 3, 3.5)
+FAR_AT = 0.75
 
 
 def log2(n):
@@ -33,7 +36,22 @@
     opposite = lax.rem(place + n_tp // 2, n_tp)
     hops = n_tp // 2 - 1
     per = n_ep // CHUNKS
-    group, seat = lax.div(me, per), lax.rem(me, per)
+    core, z = lax.rem(me, CORES), lax.rem(lax.div(me, CORES), DEPTH)
+    x = lax.div(me, CORES * DEPTH)
+    layers = n_ep // DEPTH
+    layer = x * CORES + core
+    width = DEPTH // CHUNKS
+    seat = layer * width
+
+    def mate(c, i, sign):
+        steps = DISTANCES[c]
+        other = lax.rem(layer + lax.div(i, width), layers)
+        q = lax.rem(i, width)
+        far = steps[0] + q * (steps[-1] - steps[0])
+        deep = lax.rem(z + sign * far + DEPTH, DEPTH)
+        peer = (lax.div(other, CORES) * DEPTH + deep) * CORES + lax.rem(other, CORES)
+        return peer, seat + q, other * width + q
+
     top, toks = routes.shape[1], tokens.shape[0]
     rows = batches * cap
     slots = n_ep * rows
@@ -130,10 +148,10 @@
 
             @pl.loop(1 if c == 0 else 0, per)
             def _(i):
-                peer = lax.rem(group + c, CHUNKS) * per + lax.rem(seat + i, per)
+                peer, mine, _ = mate(c, i, 1)
                 pltpu.make_async_remote_copy(
                     src_ref=source.at[peer],
-                    dst_ref=gathered.at[c, slot_id, seat],
+                    dst_ref=gathered.at[c, slot_id, mine],
                     send_sem=send.at[c],
                     recv_sem=recv.at[c],
                     device_id={"ep": peer},
@@ -284,10 +302,9 @@
 
         @pl.loop(1 if c == 0 else 0, per)
         def _(i):
-            other = lax.rem(seat + i, per)
-            peer = lax.rem(group + CHUNKS - c, CHUNKS) * per + other
+            peer, _, theirs = mate(c, i, -1)
             pltpu.make_async_remote_copy(
-                src_ref=source.at[c, other],
+                src_ref=source.at[c, theirs],
                 dst_ref=target.at[me],
                 send_sem=send.at[c],
                 recv_sem=recv.at[c],

time: 107 us -> 103 us (0.963)
  Pallas kernels: 106 us -> 102 us
    pallas_call x1, Pallas kernels: 106 us -> 102 us  [shards(): pl.pallas_call(functools.partial(kernel, n_ep, n_tp, batches, cap), out_s...]
where the time goes in v3:
time: 103 us
  Pallas kernels  102 us (99%)
  local copies, waits for them, and re-layouts  1.38 us (1%)
    pallas_call x1, Pallas kernels, shards(): pl.pallas_call(functools.partial(kernel, n_ep, n_tp, batches, cap), out_s...  102 us

profile of v3, /device:TPU:1, one launch (start us, length us, event | category | flops | bytes accessed | tf_op | source)
XLA Modules:
  0.0 103.2 jit_solution(18160646614238147766)
XLA Ops:
  0.0 101.8 %expert_layer.1 = bf16[32,512]{1,0:T(8,128)(2,1)} custom-call(s32[2,8,16]{2,1,0:T(8,128)} %bitcast.12, f32[2,8,16]{2,1,0:T(8,128)} %bitcast.13, bf16[32,512]{1,0:T(8,128)(2,1)} %bitcast.11, bf16[8,512,128]{2,1,0:T(8,128)(2,1)} %bitcast.7, bf16[8,512,128]{2,1,0:T(8,128)(2,1)} %bitcast.8, bf16[128,4096]{1,0:T(8,128)(2,1)} %bitcast.9), custom_call_target="tpu_custom_call" | custom-call | tf_op jit(solution)/shard_map/expert_layer/pallas_call | solution.py:394
  101.8 1.4 %copy.8 = bf16[2,16,512]{2,1,0:T(8,128)(2,1)} copy(bf16[2,16,512]{2,1,0:T(8,128)(2,1)} %bitcast.10) | data formatting | bytes 65536

commit v4 on v3

--- a/solution.py
+++ b/solution.py
@@ -12,8 +12,8 @@
 DEPTH = 8
 CORES = 2
 CHUNKS = len(DISTANCES)
-OFFSETS = (0, 0.5, 1, 1.5, 2, 2.5, 3, 3.5)
-FAR_AT = 0.75
+OFFSETS = (0, 0.34, 0.67, 1, 1.34, 1.67, 2, 2.34)
+FAR_AT = 1.2
 
 
 def log2(n):

time: 103 us -> 104 us (level)
    pallas_call x1, Pallas kernels: 102 us -> 103 us  [shards(): pl.pallas_call(functools.partial(kernel, n_ep, n_tp, batches, cap), out_s...]
where the time goes in v4:
time: 104 us
  Pallas kernels  103 us (99%)
  local copies, waits for them, and re-layouts  1.38 us (1%)
    pallas_call x1, Pallas kernels, shards(): pl.pallas_call(functools.partial(kernel, n_ep, n_tp, batches, cap), out_s...  103 us

profile of v4, /device:TPU:1, one launch (start us, length us, event | category | flops | bytes accessed | tf_op | source)
XLA Modules:
  0.0 104.2 jit_solution(15938356565864579537)
XLA Ops:
  0.0 102.8 %expert_layer.1 = bf16[32,512]{1,0:T(8,128)(2,1)} custom-call(s32[2,8,16]{2,1,0:T(8,128)} %bitcast.12, f32[2,8,16]{2,1,0:T(8,128)} %bitcast.13, bf16[32,512]{1,0:T(8,128)(2,1)} %bitcast.11, bf16[8,512,128]{2,1,0:T(8,128)(2,1)} %bitcast.7, bf16[8,512,128]{2,1,0:T(8,128)(2,1)} %bitcast.8, bf16[128,4096]{1,0:T(8,128)(2,1)} %bitcast.9), custom_call_target="tpu_custom_call" | custom-call | tf_op jit(solution)/shard_map/expert_layer/pallas_call | solution.py:394
  102.9 1.4 %copy.8 = bf16[2,16,512]{2,1,0:T(8,128)(2,1)} copy(bf16[2,16,512]{2,1,0:T(8,128)(2,1)} %bitcast.10) | data formatting | bytes 65536
